TPU v7x, 32 devices: a whole 2x2x4 slice. The times are simulated.
32 devices in a mesh: row: 8 (over y, x, core), col: 4 (over z).
Axes of the slice: x: 2, y: 2, z: 4, core: 2. Of those that a mesh axis runs over, the one named last changes fastest.
Arguments:
- chol: bfloat16 [3, 6144, 2048], P(None, 'row', 'col'), may hold values from -0.67578125 to 0.67578125
- amps: bfloat16 [9, 2048, 2048], P(None, 'row', 'col'), may hold values from -0.19921875 to 0.19921875
- eps_occ: float32 [3], replicated, may hold values from -2 to -0.5
- eps_vir: float32 [2048], replicated, may hold values from 1 to 8
- pairs: int32 [9, 2], replicated, may hold values from 0 to 2, as said below
Outputs:
- residual: float32 [9, 2048, 2048], P(None, 'row', 'col')
Inputs may be any that keep to these rules, and one draw needn't show every extreme that they name: `pairs`: the rows list every ordered pair (i, j) of orbitals 0 to 2 exactly once.
All inputs are finite; a program needn't handle non-finite values.
Results may differ from a plain program's by a relative error of at most 0.0039.
Values may be sent and summed in bfloat16 or wider, within the bound.
A program may use at most 128 MiB of HBM per device.

v0:
```python
import jax
import jax.numpy as jnp
from jax import lax
from jax.sharding import PartitionSpec as P


def from_root(block, axis, source):
    block = jnp.where(lax.axis_index(axis) == source, block, jnp.zeros_like(block))
    return lax.psum(block, axis)


def per_device(chol, amps, eps_occ, eps_vir, pairs):
    row_index = lax.axis_index("row")
    col_index = lax.axis_index("col")
    occ = chol.shape[0]
    slabs = amps.shape[0]
    tile_rows = amps.shape[1]
    tile_cols = amps.shape[2]
    offset = row_index % 2 * tile_rows
    flat_pair = pairs[:, 0] * occ + pairs[:, 1]
    matches = (flat_pair[None, :] == jnp.arange(slabs, dtype=jnp.int32)[:, None]).astype(jnp.int32)
    slot = jnp.sum(matches * jnp.arange(slabs, dtype=jnp.int32)[None, :], axis=1)
    grid = jnp.take(amps, slot, axis=0).reshape(occ, occ, tile_rows, tile_cols)
    col_panels = lax.all_gather(chol, "row", axis=1, tiled=True)
    own_rows = lax.dynamic_slice_in_dim(col_panels, offset, tile_rows, 2)
    row_panels = from_root(own_rows, "col", row_index // 2)
    coulomb = lax.dot_general(
        row_panels, col_panels, (((1,), (1,)), ((), ())), preferred_element_type=jnp.float32
    )
    coulomb_b = coulomb.astype(jnp.bfloat16)
    left_rows = lax.all_gather(coulomb_b, "col", axis=3, tiled=True)
    left = left_rows
    dressing = lax.dot_general(
        left,
        lax.all_gather(grid, "row", axis=2, tiled=True),
        (((2, 3), (0, 2)), ((), ())),
        preferred_element_type=jnp.float32,
    )
    dressed = coulomb + dressing
    dressed_b = dressed.astype(jnp.bfloat16)
    amp_rows = lax.all_gather(grid, "col", axis=3, tiled=True)
    left = amp_rows
    quadratic = lax.dot_general(
        left,
        lax.all_gather(dressed_b, "row", axis=1, tiled=True),
        (((1, 3), (0, 1)), ((), ())),
        preferred_element_type=jnp.float32,
    )
    eps_rows = lax.dynamic_slice_in_dim(eps_vir, row_index * tile_rows, tile_rows, 0)
    eps_cols = lax.dynamic_slice_in_dim(eps_vir, col_index * tile_cols, tile_cols, 0)
    denom = (
        eps_rows[None, :, None, None]
        + eps_cols[None, None, None, :]
        - eps_occ[:, None, None, None]
        - eps_occ[None, None, :, None]
    )
    amp_float = jnp.transpose(grid, (0, 2, 1, 3)).astype(jnp.float32)
    result = denom * amp_float + dressed + quadratic
    ordered = jnp.transpose(result, (0, 2, 1, 3)).reshape(occ * occ, tile_rows, tile_cols)
    return jnp.take(ordered, flat_pair, axis=0)


def solution(mesh):
    placed = (P(None, "row", "col"), P(None, "row", "col"), P(), P(), P())
    return jax.shard_map(
        per_device, mesh=mesh, in_specs=placed, out_specs=P(None, "row", "col"), check_vma=False
    )
```

profile of v0, /device:TPU:0, one launch (start us, length us, event | category | flops | bytes accessed | tf_op | source)
XLA Modules:
  0.0 1017.2 jit_solution(9229886071944885983)
XLA Ops:
  6.5 0.7 all-gather.6.cloned.1.call-update
  7.3 103.3 %all-gather.6.cloned.1.call-done = bf16[3,6144,512]{2,1,0:T(8,128)(2,1)} async-done(((bf16[3,768,512]{2,1,0:T(8,128)(2,1)}), bf16[3,6144,512]{2,1,0:T(8,128)(2,1)}) %all-gather.6.cloned.1.call-update) | async-done | bytes 18874384 | tf_op jit(solution)/shard_map/all_gather | solution.py:24
  110.6 8.8 dynamic-slice_select_fusion
  119.5 0.6 copy-done.3
  120.1 0.1 select_reduce_fusion
  120.2 0.1 reduce_sum.14
  120.3 2.3 gather_fusion
  122.6 3.4 broadcast_select_fusion.1
  126.1 318.1 %all-reduce.2.cloned.1.call-done = bf16[3,6144,256]{2,1,0:T(8,128)(2,1)} async-done(((bf16[3,6144,256]{2,1,0:T(8,128)(2,1)}), bf16[3,6144,256]{2,1,0:T(8,128)(2,1)}) %all-reduce.2.cloned.1.call-update) | async-done | bytes 9437200 | tf_op jit(solution)/shard_map/psum | solution.py:9
  444.3 22.1 %fusion.21 = (bf16[3,256,3,512]{3,1,2,0:T(8,128)(2,1)}, f32[3,256,3,512]{3,1,2,0:T(8,128)}) fusion(bf16[3,6144,512]{2,1,0:T(8,128)(2,1)} %all-gather.6.cloned.1.call-done, bf16[3,6144,256]{2,1,0:T(8,128)(2,1)} %all-reduce.2.cloned.1.call-done), kind=kOutput, calls=%fused_computation.33 | convolution fusion | flops 14496694272 | bytes 35389440 | tf_op jit(solution)/shard_map/dot_general | solution.py:27
  466.4 0.5 all-gather.12.cloned.1.call-update
  467.0 0.2 all-gather.14.cloned.1.call-start
  467.2 76.6 %all-gather.10.cloned.1.call-done = bf16[3,3,2048,512]{3,2,1,0:T(8,128)(2,1)} async-done(((bf16[3,3,256,512]{3,2,1,0:T(8,128)(2,1)}), bf16[3,3,2048,512]{3,2,1,0:T(8,128)(2,1)}) %all-gather.10.cloned.1.call-update) | async-done | bytes 18874384 | tf_op jit(solution)/shard_map/all_gather | solution.py:35
  543.8 168.2 %all-gather.8.cloned.1.call-done = bf16[3,256,3,2048]{3,1,2,0:T(8,128)(2,1)} async-done(((bf16[3,256,3,512]{3,1,2,0:T(8,128)(2,1)}), bf16[3,256,3,2048]{3,1,2,0:T(8,128)(2,1)}) %all-gather.8.cloned.1.call-update) | async-done | bytes 9437200 | tf_op jit(solution)/shard_map/all_gather | solution.py:31
  712.0 22.5 %fusion.22 = (bf16[3,256,3,512]{3,1,2,0:T(8,128)(2,1)}, f32[3,256,3,512]{3,1,2,0:T(8,128)}) fusion(f32[3,256,3,512]{3,1,2,0:T(8,128)} %get-tuple-element.8, bf16[3,3,2048,512]{3,2,1,0:T(8,128)(2,1)} %all-gather.10.cloned.1.call-done, bf16[3,256,3,2048]{3,1,2,0:T(8,128)(2,1)} %all-gather.8.cloned.1.call-done), kind=kOutput, calls=%fused_computation.34 | convolution fusion | flops 14497873920 | bytes 40108032 | tf_op jit(solution)/shard_map/dot_general | solution.py:33
  734.5 0.9 dynamic_slice.9
  735.4 0.8 dynamic_slice.10
  736.2 0.1 broadcast_add_fusion
  736.3 1.5 broadcast_subtract_fusion
  737.8 140.5 %all-gather.12.cloned.1.call-done = bf16[3,3,256,2048]{3,2,1,0:T(8,128)(2,1)} async-done(((bf16[3,3,256,512]{3,2,1,0:T(8,128)(2,1)}), bf16[3,3,256,2048]{3,2,1,0:T(8,128)(2,1)}) %all-gather.12.cloned.1.call-update) | async-done | bytes 9437200 | tf_op jit(solution)/shard_map/all_gather | solution.py:41
  878.4 98.6 %all-gather.14.cloned.1.call-done = bf16[3,2048,3,512]{3,1,2,0:T(8,128)(2,1)} async-done(((bf16[3,256,3,512]{3,1,2,0:T(8,128)(2,1)}), bf16[3,2048,3,512]{3,1,2,0:T(8,128)(2,1)}) %all-gather.14.cloned.1.call-update) | async-done | bytes 18874384 | tf_op jit(solution)/shard_map/all_gather | solution.py:45
  976.9 22.7 %bitcast_add_fusion = f32[3,3,256,512]{3,2,1,0:T(8,128)} fusion(f32[3,256,3,512]{3,1,2,0:T(8,128)} %get-tuple-element.10, bf16[3,3,256,512]{3,2,1,0:T(8,128)(2,1)S(1)} %copy-done.2, f32[3]{0:T(128)S(1)} %copy-done.4, f32[3,256,512]{2,1,0:T(8,128)} %broadcast_subtract_fusion, bf16[3,2048,3,512]{3,1,2,0:T(8,128)(2,1)} %all-gather.14.cloned.1.call-done, ...), kind=kOutput, calls=%fused_computation.14 | convolution fusion | flops 14501412864 | bytes 41680908 | tf_op jit(solution)/shard_map/dot_general | solution.py:43
  999.6 5.3 gather_fusion.1
  1004.9 5.4 broadcast_select_fusion
  (24 shorter events, 0.3 us)
Async XLA Ops:
  6.5 113.8 %copy-start = (bf16[9,256,512]{2,1,0:T(8,128)(2,1)S(1)}, bf16[9,256,512]{2,1,0:T(8,128)(2,1)}, u32[]{:S(2)}) copy-start(bf16[9,256,512]{2,1,0:T(8,128)(2,1)} %param.6) | copy-start | bytes 7077892
  6.5 104.1 %all-gather.6.cloned.1.call-start = ((), (), s32[]{:S(2)}) async-start(), calls=%async_computation | async-start | bytes 21233664 | tf_op jit(solution)/shard_map/all_gather | solution.py:24
  7.3 437.0 %all-reduce.2.cloned.1.call-start = ((), (), s32[]{:S(2)}) async-start(), calls=%async_computation.1 | async-start | bytes 18874368 | tf_op jit(solution)/shard_map/psum | solution.py:9
  119.4 0.7 copy-start.3
  119.5 424.3 %all-gather.10.cloned.1.call-start = ((), (), s32[]{:S(2)}) async-start(), calls=%async_computation.3 | async-start | bytes 21233664 | tf_op jit(solution)/shard_map/all_gather | solution.py:35
  126.1 585.9 %all-gather.8.cloned.1.call-start = ((), (), s32[]{:S(2)}) async-start(), calls=%async_computation.2 | async-start | bytes 11796480 | tf_op jit(solution)/shard_map/all_gather | solution.py:31
  466.4 412.0 %all-gather.12.cloned.1.call-start = ((), (), s32[]{:S(2)}) async-start(), calls=%async_computation.4 | async-start | bytes 11796480 | tf_op jit(solution)/shard_map/all_gather | solution.py:41
  467.0 510.0 %all-gather.14.cloned.1.call-start = ((), (), s32[]{:S(2)}) async-start(), calls=%async_computation.5 | async-start | bytes 21233664 | tf_op jit(solution)/shard_map/all_gather | solution.py:45
  712.0 24.3 %copy-start.4 = (f32[3]{0:T(128)S(1)}, f32[3]{0:T(128)}, u32[]{:S(2)}) copy-start(f32[3]{0:T(128)} %param.7) | copy-start | bytes 40
  734.5 242.4 %copy-start.2 = (bf16[3,3,256,512]{3,2,1,0:T(8,128)(2,1)S(1)}, bf16[3,3,256,512]{3,2,1,0:T(8,128)(2,1)}, u32[]{:S(2)}) copy-start(bf16[3,3,256,512]{3,2,1,0:T(8,128)(2,1)} %broadcast_select_fusion.1) | copy-start | bytes 7077892
  1004.9 5.4 copy-start.1
Sparse Core Ops, SparseCore 0:
  9.2 101.3 all-gather.5
  119.6 324.6 all-reduce.1
  446.2 97.5 all-gather.9
  545.2 166.7 all-gather.7
  713.4 164.9 all-gather.11
  880.1 96.7 all-gather.13
where the time goes:
time: 1020 us
  waiting for transfers between devices  907 us (89%)
  matrix products  67.3 us (7%)
  other arithmetic  19.5 us (2%)
  between operations  13.5 us (1%)
    psum x1, waiting for transfers between devices, from_root(): return lax.psum(block, axis)  318 us
    all_gather x1, waiting for transfers between devices, per_device(): left_rows = lax.all_gather(coulomb_b, 'col', axis=3, tiled=True)  168 us
    all_gather x1, waiting for transfers between devices, per_device(): amp_rows = lax.all_gather(grid, 'col', axis=3, tiled=True)  141 us
    all_gather x1, waiting for transfers between devices, per_device(): col_panels = lax.all_gather(chol, 'row', axis=1, tiled=True)  103 us
    all_gather x1, waiting for transfers between devices, per_device(): lax.all_gather(dressed_b, 'row', axis=1, tiled=True)  98.6 us
    all_gather x1, waiting for transfers between devices, per_device(): lax.all_gather(grid, 'row', axis=2, tiled=True)  76.6 us
    dot_general x1, matrix products, per_device(): lax.dot_general(left, lax.all_gather(dressed_b, 'row', axis=1, tiled=True...  22.7 us
    dot_general x1, matrix products, per_device(): lax.dot_general(left, lax.all_gather(grid, 'row', axis=2, tiled=True), ((...  22.5 us
  transfers between devices with their start and end apart: 6, of which 6 were waited for; matrix products, arithmetic and copies ran while one was open for 5% of the time, Pallas kernels for 0%

commit v1 on v0

--- a/solution.py
+++ b/solution.py
@@ -38,7 +38,16 @@
     )
     dressed = coulomb + dressing
     dressed_b = dressed.astype(jnp.bfloat16)
-    amp_rows = lax.all_gather(grid, "col", axis=3, tiled=True)
+    size_here = lax.axis_size("col")
+    xs_all = [grid]
+    for i0 in range(1, size_here):
+        xs_all.append(
+            lax.ppermute(
+                xs_all[i0 - 1], "col", [(c, (c - 1) % size_here) for c in range(size_here)]
+            )
+        )
+    shaped = jnp.concatenate(xs_all, axis=3)
+    amp_rows = jnp.roll(shaped, lax.axis_index("col") * grid.shape[3], axis=3)
     left = amp_rows
     quadratic = lax.dot_general(
         left,

time: 1020 us -> 949 us (0.930)
  waiting for transfers between devices: 907 us -> 809 us
  local copies, waits for them, and re-layouts: 9.96 us -> 31.4 us
    ppermute x0 -> x3, waiting for transfers between devices: none -> 143 us  [per_device(): lax.ppermute(xs_all[i0 - 1], 'col', [(c, (c - 1) % size_here) for c in ra...]
    all_gather x1 -> x0, waiting for transfers between devices: 141 us -> none  [per_device(): amp_rows = lax.all_gather(grid, 'col', axis=3, tiled=True)]
    all_gather x1, waiting for transfers between devices: 98.6 us -> 0.01 us  [per_device(): lax.all_gather(dressed_b, 'row', axis=1, tiled=True)]
    unnamed x10 -> x20, local copies, waits for them, and re-layouts: 0.62 us -> 18.9 us
  transfers between devices with their start and end apart: 6 -> 8, of which waited for: 6 -> 7; matrix products, arithmetic and copies ran while one was open for 5% -> 6% of each run, Pallas kernels for 0% -> 0%
where the time goes in v1:
time: 949 us; the launch traced here: 948 us
  waiting for transfers between devices  809 us (85%)
  matrix products  67.7 us (7%)
  local copies, waits for them, and re-layouts  31.4 us (3%)
  other arithmetic  20.8 us (2%)
  between operations  13.2 us (1%)
    psum x1, waiting for transfers between devices, from_root(): return lax.psum(block, axis)  317 us
    all_gather x1, waiting for transfers between devices, per_device(): left_rows = lax.all_gather(coulomb_b, 'col', axis=3, tiled=True)  168 us
    ppermute x3, waiting for transfers between devices, per_device(): lax.ppermute(xs_all[i0 - 1], 'col', [(c, (c - 1) % size_here) for c in ra...  143 us
    all_gather x1, waiting for transfers between devices, per_device(): col_panels = lax.all_gather(chol, 'row', axis=1, tiled=True)  103 us
    all_gather x1, waiting for transfers between devices, per_device(): lax.all_gather(grid, 'row', axis=2, tiled=True)  77.3 us
    dot_general x1, matrix products, per_device(): lax.dot_general(left, lax.all_gather(dressed_b, 'row', axis=1, tiled=True...  22.8 us
    dot_general x1, matrix products, per_device(): lax.dot_general(left, lax.all_gather(grid, 'row', axis=2, tiled=True), ((...  22.7 us
    dot_general x1, matrix products, per_device(): lax.dot_general(row_panels, col_panels, (((1,), (1,)), ((), ())), preferr...  22.2 us
  transfers between devices with their start and end apart: 8, of which 7 were waited for; matrix products, arithmetic and copies ran while one was open for 6% of the time, Pallas kernels for 0%

profile of v1, /device:TPU:0, one launch (start us, length us, event | category | flops | bytes accessed | tf_op | source)
XLA Modules:
  0.0 948.4 jit_solution(12958245235492623053)
XLA Ops:
  7.3 103.3 %all-gather.5.cloned.1.call-done = bf16[3,6144,512]{2,1,0:T(8,128)(2,1)} async-done(((bf16[3,768,512]{2,1,0:T(8,128)(2,1)}), bf16[3,6144,512]{2,1,0:T(8,128)(2,1)}) %all-gather.5.cloned.1.call-update) | async-done | bytes 18874384 | tf_op jit(solution)/shard_map/all_gather | solution.py:24
  110.6 8.8 dynamic-slice_select_fusion
  120.3 2.3 gather_fusion
  122.6 4.8 constant_dynamic-update-slice_fusion.7
  127.5 316.7 %all-reduce.2.cloned.1.call-done = bf16[3,6144,256]{2,1,0:T(8,128)(2,1)} async-done(((bf16[3,6144,256]{2,1,0:T(8,128)(2,1)}), bf16[3,6144,256]{2,1,0:T(8,128)(2,1)}) %all-reduce.2.cloned.1.call-update) | async-done | bytes 9437200 | tf_op jit(solution)/shard_map/psum | solution.py:9
  444.3 22.2 %fusion.23 = (bf16[3,256,3,512]{3,1,2,0:T(8,128)(2,1)}, f32[3,256,3,512]{3,1,2,0:T(8,128)}) fusion(bf16[3,6144,512]{2,1,0:T(8,128)(2,1)} %all-gather.5.cloned.1.call-done, bf16[3,6144,256]{2,1,0:T(8,128)(2,1)} %all-reduce.2.cloned.1.call-done), kind=kOutput, calls=%fused_computation.43 | convolution fusion | flops 14496694272 | bytes 35389440 | tf_op jit(solution)/shard_map/dot_general | solution.py:27
  466.5 77.3 %all-gather.9.cloned.1.call-done = bf16[3,3,2048,512]{3,2,1,0:T(8,128)(2,1)} async-done(((bf16[3,3,256,512]{3,2,1,0:T(8,128)(2,1)}), bf16[3,3,2048,512]{3,2,1,0:T(8,128)(2,1)}) %all-gather.9.cloned.1.call-update) | async-done | bytes 18874384 | tf_op jit(solution)/shard_map/all_gather | solution.py:35
  543.7 168.2 %all-gather.7.cloned.1.call-done = bf16[3,256,3,2048]{3,1,2,0:T(8,128)(2,1)} async-done(((bf16[3,256,3,512]{3,1,2,0:T(8,128)(2,1)}), bf16[3,256,3,2048]{3,1,2,0:T(8,128)(2,1)}) %all-gather.7.cloned.1.call-update) | async-done | bytes 9437200 | tf_op jit(solution)/shard_map/all_gather | solution.py:31
  712.0 22.7 %fusion.24 = (bf16[3,256,3,512]{3,1,2,0:T(8,128)(2,1)}, f32[3,256,3,512]{3,1,2,0:T(8,128)}) fusion(f32[3,256,3,512]{3,1,2,0:T(8,128)} %get-tuple-element.10, bf16[3,3,2048,512]{3,2,1,0:T(8,128)(2,1)} %all-gather.9.cloned.1.call-done, bf16[3,256,3,2048]{3,1,2,0:T(8,128)(2,1)} %all-gather.7.cloned.1.call-done), kind=kOutput, calls=%fused_computation.44 | convolution fusion | flops 14497873920 | bytes 40108032 | tf_op jit(solution)/shard_map/dot_general | solution.py:33
  735.0 52.9 %collective-permute-done = bf16[3,3,256,512]{3,2,1,0:T(8,128)(2,1)S(1)} collective-permute-done((bf16[3,3,256,512]{3,2,1,0:T(8,128)(2,1)S(1)}, bf16[3,3,256,512]{3,2,1,0:T(8,128)(2,1)S(1)}, u32[]{:S(2)}, u32[]{:S(2)}) %collective-permute-start) | collective-permute-done | bytes 2359328 | tf_op jit(solution)/shard_map/ppermute | solution.py:45
  789.3 2.1 collective-permute-start.1
  791.4 50.4 %collective-permute-done.1 = bf16[3,3,256,512]{3,2,1,0:T(8,128)(2,1)} collective-permute-done((bf16[3,3,256,512]{3,2,1,0:T(8,128)(2,1)S(1)}, bf16[3,3,256,512]{3,2,1,0:T(8,128)(2,1)}, u32[]{:S(2)}, u32[]{:S(2)}) %collective-permute-start.1) | collective-permute-done | bytes 2359328 | tf_op jit(solution)/shard_map/ppermute | solution.py:45
  841.8 3.8 collective-permute-start.2
  848.7 3.5 constant_dynamic-update-slice_fusion.6
  852.1 3.4 constant_dynamic-update-slice_fusion.5
  855.5 39.4 %collective-permute-done.2 = bf16[3,3,256,512]{3,2,1,0:T(8,128)(2,1)} collective-permute-done((bf16[3,3,256,512]{3,2,1,0:T(8,128)(2,1)}, bf16[3,3,256,512]{3,2,1,0:T(8,128)(2,1)}, u32[]{:S(2)}, u32[]{:S(2)}) %collective-permute-start.2) | collective-permute-done | bytes 2359328 | tf_op jit(solution)/shard_map/ppermute | solution.py:45
  894.9 3.4 constant_dynamic-update-slice_fusion.4
  898.3 1.6 constant_dynamic-update-slice_fusion.3
  899.9 1.6 constant_dynamic-update-slice_fusion.2
  901.6 3.3 constant_dynamic-update-slice_fusion.1
  904.9 3.4 constant_dynamic-update-slice_fusion
  908.3 22.8 %bitcast_add_fusion = f32[3,3,256,512]{3,2,1,0:T(8,128)} fusion(f32[3,256,3,512]{3,1,2,0:T(8,128)} %get-tuple-element.12, bf16[3,3,256,512]{3,2,1,0:T(8,128)(2,1)S(1)} %copy-done.2, f32[3]{0:T(128)S(1)} %copy-done.6, f32[3,256,512]{2,1,0:T(8,128)} %broadcast_subtract_fusion, bf16[3,2048,3,512]{3,1,2,0:T(8,128)(2,1)} %all-gather.11.cloned.1.call-done, ...), kind=kOutput, calls=%fused_computation.15 | convolution fusion | flops 14501412864 | bytes 41680912 | tf_op jit(solution)/shard_map/dot_general | solution.py:52
  931.1 5.3 gather_fusion.1
  936.4 5.4 broadcast_select_fusion
  (38 shorter events, 6.6 us)
Async XLA Ops:
  6.5 113.8 %copy-start = (bf16[9,256,512]{2,1,0:T(8,128)(2,1)S(1)}, bf16[9,256,512]{2,1,0:T(8,128)(2,1)}, u32[]{:S(2)}) copy-start(bf16[9,256,512]{2,1,0:T(8,128)(2,1)} %param.6) | copy-start | bytes 7077892
  6.5 104.1 %all-gather.5.cloned.1.call-start = ((), (), s32[]{:S(2)}) async-start(), calls=%async_computation | async-start | bytes 21233664 | tf_op jit(solution)/shard_map/all_gather | solution.py:24
  7.3 437.0 %all-reduce.2.cloned.1.call-start = ((), (), s32[]{:S(2)}) async-start(), calls=%async_computation.1 | async-start | bytes 18874368 | tf_op jit(solution)/shard_map/psum | solution.py:9
  119.4 0.7 copy-start.5
  119.5 424.3 %all-gather.9.cloned.1.call-start = ((), (), s32[]{:S(2)}) async-start(), calls=%async_computation.3 | async-start | bytes 21233664 | tf_op jit(solution)/shard_map/all_gather | solution.py:35
  127.5 584.5 %all-gather.7.cloned.1.call-start = ((), (), s32[]{:S(2)}) async-start(), calls=%async_computation.2 | async-start | bytes 11796480 | tf_op jit(solution)/shard_map/all_gather | solution.py:31
  466.4 441.8 %all-gather.11.cloned.1.call-start = ((), (), s32[]{:S(2)}) async-start(), calls=%async_computation.4 | async-start | bytes 21233664 | tf_op jit(solution)/shard_map/all_gather | solution.py:54
  712.0 22.7 %copy-start.2 = (bf16[3,3,256,512]{3,2,1,0:T(8,128)(2,1)S(1)}, bf16[3,3,256,512]{3,2,1,0:T(8,128)(2,1)}, u32[]{:S(2)}) copy-start(bf16[3,3,256,512]{3,2,1,0:T(8,128)(2,1)} %get-tuple-element.8) | copy-start | bytes 7077892
  712.0 135.3 %copy-start.6 = (f32[3]{0:T(128)S(1)}, f32[3]{0:T(128)}, u32[]{:S(2)}) copy-start(f32[3]{0:T(128)} %param.7) | copy-start | bytes 40
  734.7 53.2 %collective-permute-start = (bf16[3,3,256,512]{3,2,1,0:T(8,128)(2,1)S(1)}, bf16[3,3,256,512]{3,2,1,0:T(8,128)(2,1)S(1)}, u32[]{:S(2)}, u32[]{:S(2)}) collective-permute-start(bf16[3,3,256,512]{3,2,1,0:T(8,128)(2,1)S(1)} %copy-done.2), channel_id=1, source_target_pairs={{0,3},{1,0},{2,1},{3,2},{4,7},{5,4},{6,5},{7,6},{8,11},{9,8},{10,9... | collective-permute-start | bytes 7077896 | tf_op jit(solution)/shard_map/ppermute | solution.py:45
  787.9 1.4 copy-start.3
  789.3 52.5 %collective-permute-start.1 = (bf16[3,3,256,512]{3,2,1,0:T(8,128)(2,1)S(1)}, bf16[3,3,256,512]{3,2,1,0:T(8,128)(2,1)}, u32[]{:S(2)}, u32[]{:S(2)}) collective-permute-start(bf16[3,3,256,512]{3,2,1,0:T(8,128)(2,1)S(1)} %collective-permute-done), channel_id=1, source_target_pairs={{0,3},{1,0},{2,1},{3,2},{4,7},{5,4},{6,5},{7,6},{8,11},{9,8},{10,9... | collective-permute-start | bytes 7077896 | tf_op jit(solution)/shard_map/ppermute | solution.py:45
  841.8 53.1 %collective-permute-start.2 = (bf16[3,3,256,512]{3,2,1,0:T(8,128)(2,1)}, bf16[3,3,256,512]{3,2,1,0:T(8,128)(2,1)}, u32[]{:S(2)}, u32[]{:S(2)}) collective-permute-start(bf16[3,3,256,512]{3,2,1,0:T(8,128)(2,1)} %collective-permute-done.1), channel_id=1, source_target_pairs={{0,3},{1,0},{2,1},{3,2},{4,7},{5,4},{6,5},{7,6},{8,11},{9,8},{10,9... | collective-permute-start | bytes 7077896 | tf_op jit(solution)/shard_map/ppermute | solution.py:45
  855.5 44.4 %copy-start.4 = (bf16[3,3,256,512]{3,2,1,0:T(8,128)(2,1)S(1)}, bf16[3,3,256,512]{3,2,1,0:T(8,128)(2,1)}, u32[]{:S(2)}) copy-start(bf16[3,3,256,512]{3,2,1,0:T(8,128)(2,1)} %copy-done.3) | copy-start | bytes 7077892
  936.4 5.4 copy-start.1
Sparse Core Ops, SparseCore 0:
  9.2 101.3 all-gather.4
  119.6 324.6 all-reduce.1
  446.2 97.5 all-gather.8
  545.2 166.7 all-gather.6
  734.8 96.7 all-gather.10
